TPU v7x, 32 devices: a whole 2x2x4 slice. The times are simulated.
32 devices in a mesh: jobs: 2 (over x), seq: 16 (over z, y, core).
Axes of the slice: x: 2, y: 2, z: 4, core: 2. Of those that a mesh axis runs over, the one named last changes fastest.
Arguments:
- queries: bfloat16 [1024, 4096], P(('jobs', 'seq')), parts along dimension 0, may hold values from -12 to 12
- keys: bfloat16 [1024, 4096], P(('jobs', 'seq')), parts along dimension 0, may hold values from -6 to 6
- values: bfloat16 [1024, 4096], P(('jobs', 'seq')), parts along dimension 0, may hold values from -6 to 6
- live_counts: int32 [2, 16], P('jobs', 'seq'), parts along dimension 0, may hold values from 4 to 16, as said below
- merge_dest: int32 [2, 1024], P('jobs', 'seq'), parts along dimension 0, may hold values from 0 to 15, as said below
- latents: float32 [2, 1024, 64], P('jobs', 'seq'), parts along dimension 0, may hold values from -6 to 6
- guidance: float32 [2], P('jobs'), parts along dimension 0, may hold values from 3 to 6
- step_index: int32 [2], P('jobs'), parts along dimension 0, may hold values from 0 to 980
- out_weight: bfloat16 [4096, 64], replicated, may hold values from -0.09375 to 0.09375
Outputs:
- denoised: float32 [2, 1024, 64], P('jobs', 'seq'), parts along dimension 0
- merged_next: float32 [2, 256, 64], P('jobs', 'seq'), parts along dimension 0
There are 2 independent parts, one for each index of `jobs`. A program takes and returns all parts, laid end to end along the dimension named above; an argument that names none is the same for every part. Nothing has to cross between parts.
Inputs may be any that keep to these rules, and one draw needn't show every extreme that they name: `live_counts`: in every video some merge group has exactly 16 live slots. `merge_dest`: each token names a slot of its own merge group below that group's live count, and every live slot is named by at least one token.
All inputs are finite; a program needn't handle non-finite values.
Results may differ from a plain program's by a relative error of at most 0.0031.
Values may be sent and summed in bfloat16 or wider, within the bound.
No kernel may reach another device: no remote copies, remote signals or barrier semaphores. Data moves between devices by JAX's collectives and lax.ppermute only.
A program may use at most 64 MiB of HBM per device.

v0:
```python
import math
import jax
import jax.numpy as jnp
from jax import lax
from jax.sharding import PartitionSpec as P

HEADS = 32
HD = 128
TIMESTEPS = 1000
STRIDE = 20
neg_big = -1e30
shift_value = 5.0


def sigma_of(step_value):
    frac = 1.0 - step_value / TIMESTEPS
    return shift_value * frac / (1.0 + (shift_value - 1.0) * frac)


def attend_branch(query_rows, key_rows, value_rows, key_live, score_scale):
    total_rows = query_rows.shape[0]
    block_rows = 512 if total_rows % 512 == 0 else total_rows

    def one_block(query_block):
        scores = (
            lax.dot_general(
                query_block, key_rows, (((1,), (1,)), ((), ())), preferred_element_type=jnp.float32
            )
            * score_scale
        )
        scores = jnp.where(key_live[None, :], scores, neg_big)
        row_top = jnp.max(scores, axis=-1, keepdims=True)
        weights = jnp.exp(scores - row_top)
        probabilities = (weights / jnp.sum(weights, axis=-1, keepdims=True)).astype(jnp.bfloat16)
        return jnp.dot(probabilities, value_rows, preferred_element_type=jnp.float32).astype(
            jnp.bfloat16
        )

    blocks = query_rows.reshape(total_rows // block_rows, block_rows, query_rows.shape[1])
    return lax.map(one_block, blocks).reshape(total_rows, query_rows.shape[1])


def local(
    queries, keys, values, live_counts, merge_dest, latents, guidance, step_index, out_weight
):
    groups = lax.axis_size("seq")
    device = lax.axis_index("seq")
    pair_count = groups // 2
    local_rows, columns = queries.shape
    cap_half = local_rows // 2
    videos = guidance.shape[0]
    feature_width = columns // videos
    per_device = columns // groups
    item_count = per_device // HD
    branch_slots = groups * cap_half
    score_scale = 1.0 / math.sqrt(HD)
    counts_all = lax.all_gather(live_counts, "seq", axis=1, tiled=True)
    query_in, key_in, value_in = (
        lax.all_to_all(queries, "seq", split_axis=1, concat_axis=0, tiled=True),
        lax.all_to_all(keys, "seq", split_axis=1, concat_axis=0, tiled=True),
        lax.all_to_all(values, "seq", split_axis=1, concat_axis=0, tiled=True),
    )
    count_grid = counts_all.reshape(videos, 2, pair_count).transpose(0, 2, 1)
    live_slots = (
        jnp.arange(cap_half, dtype=jnp.int32)[None, None, None, :] < count_grid[..., None]
    ).reshape(videos, branch_slots)
    guided_parts = []
    head_numbers = []
    for item_index in range(item_count):
        global_item = device * item_count + item_index
        video_index = global_item // HEADS
        key_live = live_slots[video_index]
        col_start = item_index * HD
        branch_outs = []
        for branch_no in range(2):
            row_start = branch_no * branch_slots
            branch_outs.append(
                attend_branch(
                    query_in[row_start : row_start + branch_slots, col_start : col_start + HD],
                    key_in[row_start : row_start + branch_slots, col_start : col_start + HD],
                    value_in[row_start : row_start + branch_slots, col_start : col_start + HD],
                    key_live,
                    score_scale,
                )
            )
        conditioned = branch_outs[0].astype(jnp.float32)
        uncond = branch_outs[1].astype(jnp.float32)
        guided_parts.append(
            (uncond + guidance[video_index] * (conditioned - uncond)).astype(jnp.bfloat16)
        )
        head_numbers.append(global_item % HEADS)
    stacked = jnp.concatenate(guided_parts, axis=1)
    ordered = (
        stacked.reshape(pair_count, 2, cap_half, per_device)
        .transpose(1, 0, 2, 3)
        .reshape(groups * cap_half, per_device)
    )
    mixed = lax.all_to_all(ordered, "seq", split_axis=0, concat_axis=1, tiled=True)
    merged = jnp.einsum(
        "jva,ac->vjc",
        mixed.reshape(cap_half, videos, feature_width),
        out_weight,
        preferred_element_type=jnp.float32,
    )
    onehot = (merge_dest[..., None] == jnp.arange(cap_half, dtype=jnp.int32)).astype(jnp.float32)
    velocity = jnp.einsum("vrj,vjc->vrc", onehot, merged, precision=lax.Precision.HIGHEST)
    step_value = step_index.astype(jnp.float32)
    sigma_now = sigma_of(step_value)
    sigma_next = sigma_of(step_value + float(STRIDE))
    denoised = latents - sigma_now[:, None, None] * velocity
    advanced = latents + (sigma_next - sigma_now)[:, None, None] * velocity
    slot_sums = jnp.einsum("vrj,vrc->vjc", onehot, advanced, precision=lax.Precision.HIGHEST)
    slot_tally = jnp.sum(onehot, axis=1)
    merged_next = slot_sums / jnp.maximum(slot_tally, 1.0)[..., None]
    return (denoised, merged_next)


def solution(mesh):
    placed = (
        P(("jobs", "seq"), None),
        P(("jobs", "seq"), None),
        P(("jobs", "seq"), None),
        P("jobs", "seq"),
        P("jobs", "seq"),
        P("jobs", "seq", None),
        P("jobs"),
        P("jobs"),
        P(),
    )
    return jax.shard_map(
        local,
        mesh=mesh,
        in_specs=placed,
        out_specs=(P("jobs", "seq", None), P("jobs", "seq", None)),
        check_vma=False,
    )
```

profile of v0, /device:TPU:0, one launch (start us, length us, event | category | flops | bytes accessed | tf_op | source)
XLA Modules:
  0.0 69.5 jit_solution(11512666287636155792)
XLA Ops:
  0.6 0.0 copy-start
  0.6 1.7 %copy.78 = bf16[4,16,8,256]{3,2,0,1:T(8,128)(2,1)} copy(bf16[4,16,8,256]{3,2,1,0:T(8,128)(2,1)} %bitcast.66) | data formatting | bytes 524288 | tf_op jit(solution)/shard_map/all_to_all | solution.py:59
  2.4 0.0 copy-start.1
  2.4 7.5 %all-to-all-start = ((bf16[32,16,256]{2,0,1:T(8,128)(2,1)}), bf16[32,16,256]{2,0,1:T(8,128)(2,1)S(1)}, u32[]{:S(2)}, u32[]{:S(2)}) async-start(bf16[32,16,256]{2,0,1:T(8,128)(2,1)} %bitcast.62), calls=%async_computation | async-start | bytes 524288 | tf_op jit(solution)/shard_map/all_to_all | solution.py:59
  9.9 0.0 copy-done.1
  9.9 0.7 %copy.77 = bf16[4,16,8,256]{3,2,0,1:T(8,128)(2,1)} copy(bf16[4,16,8,256]{3,2,1,0:T(8,128)(2,1)S(1)} %bitcast.67) | data formatting | bytes 524288 | tf_op jit(solution)/shard_map/all_to_all | solution.py:60
  10.7 9.3 %all-to-all-done = bf16[32,16,256]{2,0,1:T(8,128)(2,1)S(1)} async-done(((bf16[32,16,256]{2,0,1:T(8,128)(2,1)}), bf16[32,16,256]{2,0,1:T(8,128)(2,1)S(1)}, u32[]{:S(2)}, u32[]{:S(2)}) %all-to-all-start) | async-done | bytes 262176 | tf_op jit(solution)/shard_map/all_to_all | solution.py:59
  19.9 0.0 copy-start.2
  19.9 3.7 %all-to-all-start.1 = ((bf16[32,16,256]{2,0,1:T(8,128)(2,1)}), bf16[32,16,256]{2,0,1:T(8,128)(2,1)S(1)}, u32[]{:S(2)}, u32[]{:S(2)}) async-start(bf16[32,16,256]{2,0,1:T(8,128)(2,1)} %bitcast.61), calls=%async_computation.1 | async-start | bytes 524288 | tf_op jit(solution)/shard_map/all_to_all | solution.py:60
  24.3 0.0 copy-start.5
  24.3 0.6 copy-done.5
  24.9 0.6 dynamic-slice.4
  25.5 0.7 bitcast_dynamic-update-slice_fusion
  26.2 12.4 %all-reduce = s32[16]{0:T(128)S(1)} all-reduce(s32[16]{0:T(128)S(1)} %bitcast_dynamic-update-slice_fusion), channel_id=1, replica_groups=mesh['jobs'=2,'seq'=16] {'seq'}, use_global_device_ids=true, to_apply=%add | all-reduce | flops 16 | bytes 128
  38.6 0.1 reshape.221
  38.7 0.1 copy.42
  38.7 0.1 iota_compare_fusion.4
  38.8 0.1 lt.36
  38.9 0.0 copy-done.2
  38.9 0.7 %copy.76 = bf16[4,16,8,256]{3,2,0,1:T(8,128)(2,1)} copy(bf16[4,16,8,256]{3,2,1,0:T(8,128)(2,1)S(1)} %bitcast.68) | data formatting | bytes 524288 | tf_op jit(solution)/shard_map/all_to_all | solution.py:61
  40.3 0.0 all-to-all-done.1
  40.3 3.5 %all-to-all-start.2 = ((bf16[32,16,256]{2,0,1:T(8,128)(2,1)}), bf16[32,16,256]{2,0,1:T(8,128)(2,1)S(1)}, u32[]{:S(2)}, u32[]{:S(2)}) async-start(bf16[32,16,256]{2,0,1:T(8,128)(2,1)} %bitcast.60), calls=%async_computation.2 | async-start | bytes 524288 | tf_op jit(solution)/shard_map/all_to_all | solution.py:61
  43.9 0.2 fusion.35
  44.1 0.2 fusion.36
  44.3 0.1 fusion.8
  44.4 0.2 fusion.37
  44.6 0.2 fusion.38
  44.8 9.0 %all-to-all-done.2 = bf16[32,16,256]{2,0,1:T(8,128)(2,1)S(1)} async-done(((bf16[32,16,256]{2,0,1:T(8,128)(2,1)}), bf16[32,16,256]{2,0,1:T(8,128)(2,1)S(1)}, u32[]{:S(2)}, u32[]{:S(2)}) %all-to-all-start.2) | async-done | bytes 262176 | tf_op jit(solution)/shard_map/all_to_all | solution.py:61
  53.8 0.2 convolution_convert_fusion
  54.1 0.1 fusion.7
  54.2 0.2 convolution_convert_fusion.1
  54.4 0.1 fusion.6
  54.5 0.2 convolution_convert_fusion.2
  54.7 0.1 fusion.5
  54.8 0.2 convolution_convert_fusion.3
  55.1 0.1 fusion.11
  55.1 0.7 pad_maximum_fusion
  55.8 3.5 %all-to-all-start.3 = ((bf16[16,16,256]{2,1,0:T(8,128)(2,1)}), bf16[16,16,256]{2,1,0:T(8,128)(2,1)S(1)}, u32[]{:S(2)}, u32[]{:S(2)}) async-start(bf16[16,16,256]{2,1,0:T(8,128)(2,1)} %bitcast.23), calls=%async_computation.3 | async-start | bytes 262144 | tf_op jit(solution)/shard_map/all_to_all | solution.py:98
  59.3 0.0 copy-start.4
  59.3 0.6 copy-done.4
  59.9 0.1 convert_reduce_fusion
  60.8 6.3 %all-to-all-done.3 = bf16[16,16,256]{2,1,0:T(8,128)(2,1)S(1)} async-done(((bf16[16,16,256]{2,1,0:T(8,128)(2,1)}), bf16[16,16,256]{2,1,0:T(8,128)(2,1)S(1)}, u32[]{:S(2)}, u32[]{:S(2)}) %all-to-all-start.3) | async-done | bytes 131104 | tf_op jit(solution)/shard_map/all_to_all | solution.py:98
  67.2 0.0 copy-done
  67.2 0.0 copy-start.3
  67.2 0.2 fusion.39
  67.4 0.5 copy-done.3
  67.9 0.8 %bitcast_subtract_fusion = (f32[1,64,64]{2,1,0:T(8,128)}, f32[64,64]{1,0:T(8,128)S(1)}) fusion(f32[1,64,64]{2,1,0:T(8,128)S(1)} %copy-done.3, f32[]{:T(128)} %bitcast, f32[16,64]{1,0:T(8,128)S(1)} %fusion.39, s32[64]{0:T(128)S(1)} %bitcast.86), kind=kOutput, calls=%fused_computation.52 | convolution fusion | flops 795648 | bytes 53508 | tf_op jit(solution)/shard_map/vrj,vjc->vrc/dot_general | solution.py:106
  68.8 0.7 %fusion.4 = f32[1,16,64]{2,1,0:T(8,128)} fusion(f32[1,64,64]{2,1,0:T(8,128)S(1)} %copy-done.3, f32[64,64]{1,0:T(8,128)S(1)} %get-tuple-element.65, f32[]{:T(128)} %bitcast.27, f32[16]{0:T(128)S(1)} %broadcast_maximum_fusion, s32[64]{0:T(128)S(1)} %bitcast.87), kind=kOutput, calls=%fused_computation.13 | convolution fusion | flops 796672 | bytes 37188 | tf_op jit(solution)/shard_map/vrj,vrc->vjc/dot_general | solution.py:112
  (3 shorter events, 0.0 us)
Async XLA Ops:
  0.6 66.5 %copy-start = (bf16[4096,64]{0,1:T(8,128)(2,1)S(1)}, bf16[4096,64]{0,1:T(8,128)(2,1)}, u32[]{:S(2)}) copy-start(bf16[4096,64]{0,1:T(8,128)(2,1)} %param.17) | copy-start | bytes 1572868
  2.4 7.6 %copy-start.1 = (bf16[32,4096]{1,0:T(8,128)(2,1)S(1)}, bf16[32,4096]{1,0:T(8,128)(2,1)}, u32[]{:S(2)}) copy-start(bf16[32,4096]{1,0:T(8,128)(2,1)} %param.10) | copy-start | bytes 786436
  2.4 17.6 %all-to-all-start = ((bf16[32,16,256]{2,0,1:T(8,128)(2,1)}), bf16[32,16,256]{2,0,1:T(8,128)(2,1)S(1)}, u32[]{:S(2)}, u32[]{:S(2)}) async-start(bf16[32,16,256]{2,0,1:T(8,128)(2,1)} %bitcast.62), calls=%async_computation | async-start | bytes 524288 | tf_op jit(solution)/shard_map/all_to_all | solution.py:59
  19.9 19.0 %copy-start.2 = (bf16[32,4096]{1,0:T(8,128)(2,1)S(1)}, bf16[32,4096]{1,0:T(8,128)(2,1)}, u32[]{:S(2)}) copy-start(bf16[32,4096]{1,0:T(8,128)(2,1)} %param.11) | copy-start | bytes 786436
  19.9 20.4 %all-to-all-start.1 = ((bf16[32,16,256]{2,0,1:T(8,128)(2,1)}), bf16[32,16,256]{2,0,1:T(8,128)(2,1)S(1)}, u32[]{:S(2)}, u32[]{:S(2)}) async-start(bf16[32,16,256]{2,0,1:T(8,128)(2,1)} %bitcast.61), calls=%async_computation.1 | async-start | bytes 524288 | tf_op jit(solution)/shard_map/all_to_all | solution.py:60
  24.3 0.7 copy-start.5
  40.3 13.5 %all-to-all-start.2 = ((bf16[32,16,256]{2,0,1:T(8,128)(2,1)}), bf16[32,16,256]{2,0,1:T(8,128)(2,1)S(1)}, u32[]{:S(2)}, u32[]{:S(2)}) async-start(bf16[32,16,256]{2,0,1:T(8,128)(2,1)} %bitcast.60), calls=%async_computation.2 | async-start | bytes 524288 | tf_op jit(solution)/shard_map/all_to_all | solution.py:61
  55.8 11.4 %all-to-all-start.3 = ((bf16[16,16,256]{2,1,0:T(8,128)(2,1)}), bf16[16,16,256]{2,1,0:T(8,128)(2,1)S(1)}, u32[]{:S(2)}, u32[]{:S(2)}) async-start(bf16[16,16,256]{2,1,0:T(8,128)(2,1)} %bitcast.23), calls=%async_computation.3 | async-start | bytes 262144 | tf_op jit(solution)/shard_map/all_to_all | solution.py:98
  59.3 0.7 copy-start.4
  67.2 0.8 %copy-start.3 = (f32[1,64,64]{2,1,0:T(8,128)S(1)}, f32[1,64,64]{2,1,0:T(8,128)}, u32[]{:S(2)}) copy-start(f32[1,64,64]{2,1,0:T(8,128)} %param.14) | copy-start | bytes 49156
where the time goes:
time: 70.2 us; the launch traced here: 69.5 us
  waiting for transfers between devices  24.6 us (35%)
  starting transfers between devices  18.3 us (26%)
  blocking collectives  12.4 us (18%)
  local copies, waits for them, and re-layouts  6.53 us (9%)
  matrix products  3.66 us (5%)
  between operations  2.84 us (4%)
  other arithmetic  1.2 us (2%)
    unnamed x1, blocking collectives  12.4 us
    all_to_all x1, waiting for transfers between devices, local(): lax.all_to_all(queries, 'seq', split_axis=1, concat_axis=0, tiled=True)  9.28 us
    all_to_all x1, waiting for transfers between devices, local(): lax.all_to_all(values, 'seq', split_axis=1, concat_axis=0, tiled=True)  9.02 us
    all_to_all x1, starting transfers between devices, local(): lax.all_to_all(queries, 'seq', split_axis=1, concat_axis=0, tiled=True)  7.55 us
    all_to_all x1, waiting for transfers between devices, local(): lax.all_to_all(ordered, 'seq', split_axis=0, concat_axis=1, tiled=True)  6.34 us
    all_to_all x1, starting transfers between devices, local(): lax.all_to_all(keys, 'seq', split_axis=1, concat_axis=0, tiled=True)  3.66 us
    all_to_all x1, starting transfers between devices, local(): lax.all_to_all(values, 'seq', split_axis=1, concat_axis=0, tiled=True)  3.54 us
    all_to_all x1, starting transfers between devices, local(): lax.all_to_all(ordered, 'seq', split_axis=0, concat_axis=1, tiled=True)  3.51 us
  transfers between devices with their start and end apart: 4, of which 3 were waited for; matrix products, arithmetic and copies ran while one was open for 6% of the time, Pallas kernels for 0%

commit v1 on v0

--- a/solution.py
+++ b/solution.py
@@ -95,7 +95,10 @@
         .transpose(1, 0, 2, 3)
         .reshape(groups * cap_half, per_device)
     )
-    mixed = lax.all_to_all(ordered, "seq", split_axis=0, concat_axis=1, tiled=True)
+    mixed = jnp.concatenate(
+        lax.all_to_all(jnp.stack(jnp.split(ordered, lax.axis_size("seq"), axis=0)), "seq", 0, 0),
+        axis=1,
+    )
     merged = jnp.einsum(
         "jva,ac->vjc",
         mixed.reshape(cap_half, videos, feature_width),

time: 70.2 us -> 79.1 us (1.13)
  local copies, waits for them, and re-layouts: 6.53 us -> 16 us
    unnamed x15 -> x30, local copies, waits for them, and re-layouts: 3.08 us -> 12 us
  transfers between devices with their start and end apart: 4 -> 4, of which waited for: 3 -> 3; matrix products, arithmetic and copies ran while one was open for 6% -> 5% of each run, Pallas kernels for 0% -> 0%
where the time goes in v1:
time: 79.1 us; the launch traced here: 78.4 us
  waiting for transfers between devices  24.6 us (31%)
  starting transfers between devices  18.3 us (23%)
  local copies, waits for them, and re-layouts  16 us (20%)
  blocking collectives  12.4 us (16%)
  matrix products  3.66 us (5%)
  between operations  2.85 us (4%)
    unnamed x1, blocking collectives  12.4 us
    unnamed x30, local copies, waits for them, and re-layouts  12 us
    all_to_all x1, waiting for transfers between devices, local(): lax.all_to_all(queries, 'seq', split_axis=1, concat_axis=0, tiled=True)  9.28 us
    all_to_all x1, waiting for transfers between devices, local(): lax.all_to_all(values, 'seq', split_axis=1, concat_axis=0, tiled=True)  9.02 us
    all_to_all x1, starting transfers between devices, local(): lax.all_to_all(queries, 'seq', split_axis=1, concat_axis=0, tiled=True)  7.55 us
    all_to_all x1, waiting for transfers between devices, local(): lax.all_to_all(jnp.stack(jnp.split(ordered, lax.axis_size('seq'), axis=0)...  6.34 us
    all_to_all x1, starting transfers between devices, local(): lax.all_to_all(keys, 'seq', split_axis=1, concat_axis=0, tiled=True)  3.66 us
    all_to_all x1, starting transfers between devices, local(): lax.all_to_all(values, 'seq', split_axis=1, concat_axis=0, tiled=True)  3.54 us
  transfers between devices with their start and end apart: 4, of which 3 were waited for; matrix products, arithmetic and copies ran while one was open for 5% of the time, Pallas kernels for 0%

profile of v1, /device:TPU:0, one launch (start us, length us, event | category | flops | bytes accessed | tf_op | source)
XLA Modules:
  0.0 78.4 jit_solution(7851215365985310574)
XLA Ops:
  0.6 1.7 %copy.78 = bf16[4,16,8,256]{3,2,0,1:T(8,128)(2,1)} copy(bf16[4,16,8,256]{3,2,1,0:T(8,128)(2,1)} %bitcast.146) | data formatting | bytes 524288 | tf_op jit(solution)/shard_map/all_to_all | solution.py:59
  2.4 7.5 %all-to-all-start = ((bf16[32,16,256]{2,0,1:T(8,128)(2,1)}), bf16[32,16,256]{2,0,1:T(8,128)(2,1)S(1)}, u32[]{:S(2)}, u32[]{:S(2)}) async-start(bf16[32,16,256]{2,0,1:T(8,128)(2,1)} %bitcast.126), calls=%async_computation | async-start | bytes 524288 | tf_op jit(solution)/shard_map/all_to_all | solution.py:59
  9.9 0.7 copy.77
  10.7 9.3 %all-to-all-done = bf16[32,16,256]{2,0,1:T(8,128)(2,1)S(1)} async-done(((bf16[32,16,256]{2,0,1:T(8,128)(2,1)}), bf16[32,16,256]{2,0,1:T(8,128)(2,1)S(1)}, u32[]{:S(2)}, u32[]{:S(2)}) %all-to-all-start) | async-done | bytes 262176 | tf_op jit(solution)/shard_map/all_to_all | solution.py:59
  19.9 3.7 %all-to-all-start.1 = ((bf16[32,16,256]{2,0,1:T(8,128)(2,1)}), bf16[32,16,256]{2,0,1:T(8,128)(2,1)S(1)}, u32[]{:S(2)}, u32[]{:S(2)}) async-start(bf16[32,16,256]{2,0,1:T(8,128)(2,1)} %bitcast.125), calls=%async_computation.1 | async-start | bytes 524288 | tf_op jit(solution)/shard_map/all_to_all | solution.py:60
  24.3 0.6 copy-done.5
  24.9 0.6 dynamic-slice.4
  25.5 0.7 bitcast_dynamic-update-slice_fusion
  26.2 12.4 %all-reduce = s32[16]{0:T(128)S(1)} all-reduce(s32[16]{0:T(128)S(1)} %bitcast_dynamic-update-slice_fusion), channel_id=1, replica_groups=mesh['jobs'=2,'seq'=16] {'seq'}, use_global_device_ids=true, to_apply=%add | all-reduce | flops 16 | bytes 128
  38.6 0.1 reshape.220
  38.7 0.1 copy.42
  38.7 0.1 iota_compare_fusion.4
  38.8 0.1 lt.36
  38.9 0.7 copy.76
  40.3 3.5 %all-to-all-start.2 = ((bf16[32,16,256]{2,0,1:T(8,128)(2,1)}), bf16[32,16,256]{2,0,1:T(8,128)(2,1)S(1)}, u32[]{:S(2)}, u32[]{:S(2)}) async-start(bf16[32,16,256]{2,0,1:T(8,128)(2,1)} %bitcast.124), calls=%async_computation.2 | async-start | bytes 524288 | tf_op jit(solution)/shard_map/all_to_all | solution.py:61
  43.9 0.2 fusion.35
  44.1 0.2 fusion.36
  44.4 0.2 fusion.37
  44.6 0.2 fusion.38
  44.8 9.0 %all-to-all-done.2 = bf16[32,16,256]{2,0,1:T(8,128)(2,1)S(1)} async-done(((bf16[32,16,256]{2,0,1:T(8,128)(2,1)}), bf16[32,16,256]{2,0,1:T(8,128)(2,1)S(1)}, u32[]{:S(2)}, u32[]{:S(2)}) %all-to-all-start.2) | async-done | bytes 262176 | tf_op jit(solution)/shard_map/all_to_all | solution.py:61
  53.8 0.2 convolution_convert_fusion
  54.2 0.2 convolution_convert_fusion.1
  54.5 0.2 convolution_convert_fusion.2
  54.8 0.2 convolution_convert_fusion.3
  55.1 0.6 constant_dynamic-update-slice_fusion.15
  55.7 0.6 constant_dynamic-update-slice_fusion.14
  56.3 0.6 constant_dynamic-update-slice_fusion.13
  56.9 0.6 constant_dynamic-update-slice_fusion.12
  57.5 0.6 constant_dynamic-update-slice_fusion.11
  58.1 0.6 constant_dynamic-update-slice_fusion.10
  58.7 0.6 constant_dynamic-update-slice_fusion.9
  59.3 0.6 constant_dynamic-update-slice_fusion.8
  59.9 0.6 constant_dynamic-update-slice_fusion.7
  60.5 0.6 constant_dynamic-update-slice_fusion.6
  61.1 0.6 constant_dynamic-update-slice_fusion.5
  61.7 0.6 constant_dynamic-update-slice_fusion.4
  62.3 0.6 constant_dynamic-update-slice_fusion.3
  62.9 0.6 constant_dynamic-update-slice_fusion.2
  63.5 0.6 constant_dynamic-update-slice_fusion.1
  64.1 0.6 constant_dynamic-update-slice_fusion
  64.7 3.5 %all-to-all-start.3 = ((bf16[16,16,256]{2,1,0:T(8,128)(2,1)}), bf16[16,16,256]{2,1,0:T(8,128)(2,1)S(1)}, u32[]{:S(2)}, u32[]{:S(2)}) async-start(bf16[16,16,256]{2,1,0:T(8,128)(2,1)} %constant_dynamic-update-slice_fusion), calls=%async_computation.3 | async-start | bytes 262144 | tf_op jit(solution)/shard_map/all_to_all | solution.py:99
  68.2 0.6 copy-done.4
  68.8 0.1 convert_reduce_fusion
  69.7 6.3 %all-to-all-done.3 = bf16[16,16,256]{2,1,0:T(8,128)(2,1)S(1)} async-done(((bf16[16,16,256]{2,1,0:T(8,128)(2,1)}), bf16[16,16,256]{2,1,0:T(8,128)(2,1)S(1)}, u32[]{:S(2)}, u32[]{:S(2)}) %all-to-all-start.3) | async-done | bytes 131104 | tf_op jit(solution)/shard_map/all_to_all | solution.py:99
  76.1 0.2 fusion.39
  76.3 0.5 copy-done.3
  76.8 0.8 %bitcast_subtract_fusion = (f32[1,64,64]{2,1,0:T(8,128)}, f32[64,64]{1,0:T(8,128)S(1)}) fusion(f32[1,64,64]{2,1,0:T(8,128)S(1)} %copy-done.3, f32[]{:T(128)} %bitcast, f32[16,64]{1,0:T(8,128)S(1)} %fusion.39, s32[64]{0:T(128)S(1)} %bitcast.166), kind=kOutput, calls=%fused_computation.68 | convolution fusion | flops 795648 | bytes 53508 | tf_op jit(solution)/shard_map/vrj,vjc->vrc/dot_general | solution.py:109
  77.7 0.7 fusion.4
  (19 shorter events, 0.4 us)
Async XLA Ops:
  0.6 75.4 %copy-start = (bf16[4096,64]{0,1:T(8,128)(2,1)S(1)}, bf16[4096,64]{0,1:T(8,128)(2,1)}, u32[]{:S(2)}) copy-start(bf16[4096,64]{0,1:T(8,128)(2,1)} %param.17) | copy-start | bytes 1572868
  2.4 7.6 %copy-start.1 = (bf16[32,4096]{1,0:T(8,128)(2,1)S(1)}, bf16[32,4096]{1,0:T(8,128)(2,1)}, u32[]{:S(2)}) copy-start(bf16[32,4096]{1,0:T(8,128)(2,1)} %param.10) | copy-start | bytes 786436
  2.4 17.6 %all-to-all-start = ((bf16[32,16,256]{2,0,1:T(8,128)(2,1)}), bf16[32,16,256]{2,0,1:T(8,128)(2,1)S(1)}, u32[]{:S(2)}, u32[]{:S(2)}) async-start(bf16[32,16,256]{2,0,1:T(8,128)(2,1)} %bitcast.126), calls=%async_computation | async-start | bytes 524288 | tf_op jit(solution)/shard_map/all_to_all | solution.py:59
  19.9 19.0 %copy-start.2 = (bf16[32,4096]{1,0:T(8,128)(2,1)S(1)}, bf16[32,4096]{1,0:T(8,128)(2,1)}, u32[]{:S(2)}) copy-start(bf16[32,4096]{1,0:T(8,128)(2,1)} %param.11) | copy-start | bytes 786436
  19.9 20.4 %all-to-all-start.1 = ((bf16[32,16,256]{2,0,1:T(8,128)(2,1)}), bf16[32,16,256]{2,0,1:T(8,128)(2,1)S(1)}, u32[]{:S(2)}, u32[]{:S(2)}) async-start(bf16[32,16,256]{2,0,1:T(8,128)(2,1)} %bitcast.125), calls=%async_computation.1 | async-start | bytes 524288 | tf_op jit(solution)/shard_map/all_to_all | solution.py:60
  24.3 0.7 copy-start.5
  40.3 13.5 %all-to-all-start.2 = ((bf16[32,16,256]{2,0,1:T(8,128)(2,1)}), bf16[32,16,256]{2,0,1:T(8,128)(2,1)S(1)}, u32[]{:S(2)}, u32[]{:S(2)}) async-start(bf16[32,16,256]{2,0,1:T(8,128)(2,1)} %bitcast.124), calls=%async_computation.2 | async-start | bytes 524288 | tf_op jit(solution)/shard_map/all_to_all | solution.py:61
  64.7 11.4 %all-to-all-start.3 = ((bf16[16,16,256]{2,1,0:T(8,128)(2,1)}), bf16[16,16,256]{2,1,0:T(8,128)(2,1)S(1)}, u32[]{:S(2)}, u32[]{:S(2)}) async-start(bf16[16,16,256]{2,1,0:T(8,128)(2,1)} %constant_dynamic-update-slice_fusion), calls=%async_computation.3 | async-start | bytes 262144 | tf_op jit(solution)/shard_map/all_to_all | solution.py:99
  68.2 0.7 copy-start.4
  76.1 0.8 copy-start.3
